TPU v7x, 32 devices: a whole 2x2x4 slice. The times are simulated.
32 devices in a mesh: rel: 4 (over y, x), node: 4 (over z), feat: 2 (over core).
Axes of the slice: x: 2, y: 2, z: 4, core: 2. Of those that a mesh axis runs over, the one named last changes fastest.
Arguments:
- features: float32 [3072, 768], P('node', 'feat'), may hold values from -6 to 6
- tile_values: float32 [4, 12, 12, 256, 256], P('rel', 'node'), may hold values from -0.4375 to 0.4375
- tile_cols: int32 [4, 12, 12], P('rel', 'node'), may hold values from 0 to 11, as said below
- tile_count: int32 [4, 12], P('rel', 'node'), may hold values from 1 to 12, as said below
- degree: int32 [4, 3072], P('rel', 'node'), may hold values from 1 to 16
- proj_weight: float32 [4, 768, 512], P('rel', 'feat'), may hold values from -0.21875 to 0.21875
- proj_bias: float32 [4, 512], P('rel', 'feat'), may hold values from -3 to 3
Outputs:
- metapath_out: float32 [4, 3072, 512], P(None, ('node', 'rel'), 'feat')
Inputs may be any that keep to these rules, and one draw needn't show every extreme that they name: `tile_cols`: within one row of tiles the 12 column tiles are distinct; slots at or past the count hold valid tile numbers that are not used. `tile_count`: in every relation some row of tiles has exactly 12 live slots.
All inputs are finite; a program needn't handle non-finite values.
Results may differ from a plain program's by a relative error of at most 0.0001.
Values sent between devices are 32-bit elements; how exact they have to be, the bound alone decides.
A program may use at most 128 MiB of HBM per device.

v0:
```python
import jax
import jax.numpy as jnp
from jax import lax
from jax.sharding import PartitionSpec as P


def spread(gathered, masked, col_tiles):
    columns = gathered.shape[1]
    tile_rows = gathered.reshape(-1, masked.shape[2], columns)
    sources = jnp.take(tile_rows, col_tiles, axis=0)
    summed = jnp.einsum(
        "tkab,tkbw->taw",
        masked,
        sources,
        precision=lax.Precision.HIGH,
        preferred_element_type=jnp.float32,
    )
    return summed.reshape(-1, columns)


def on_device(features, tile_values, tile_cols, tile_count, degree, proj_weight, proj_bias):
    row_scale = lax.rsqrt(degree[0].astype(jnp.float32))[:, None]
    counts = tile_count[0]
    live_mask = (jnp.arange(tile_values.shape[2])[None, :] < counts[:, None]).astype(jnp.float32)
    masked = tile_values[0] * live_mask[:, :, None, None]
    col_tiles = tile_cols[0]
    partial_sum = jnp.dot(
        features, proj_weight[0], precision=lax.Precision.HIGH, preferred_element_type=jnp.float32
    )
    current = lax.psum_scatter(partial_sum, "feat", scatter_dimension=1, tiled=True)
    for hop_index in range(2):
        gathered = lax.all_gather(row_scale * current, "node", axis=0, tiled=True)
        current = row_scale * spread(gathered, masked, col_tiles)
    result = current + proj_bias[0][None, :]
    return lax.all_to_all(result[None], "rel", split_axis=1, concat_axis=0, tiled=True)


def solution(mesh):
    return jax.shard_map(
        on_device,
        mesh=mesh,
        in_specs=(
            P("node", "feat"),
            P("rel", "node", None, None, None),
            P("rel", "node", None),
            P("rel", "node"),
            P("rel", "node"),
            P("rel", "feat", None),
            P("rel", "feat"),
        ),
        out_specs=P(None, ("node", "rel"), "feat"),
        check_vma=False,
    )
```

profile of v0, /device:TPU:0, one launch (start us, length us, event | category | flops | bytes accessed | tf_op | source)
XLA Modules:
  0.0 216.2 jit_solution(5188851948771330307)
XLA Ops:
  6.5 1.3 copy-done
  7.8 3.7 %fusion.11 = f32[768,512]{1,0:T(8,128)} fusion(f32[768,384]{1,0:T(8,128)S(1)} %copy-done, f32[1,384,512]{2,1,0:T(8,128)} %param.14), kind=kOutput, calls=%fused_computation.15 | convolution fusion | flops 905969664 | bytes 3538944 | tf_op jit(solution)/shard_map/dot_general | solution.py:27
  11.5 0.0 reduce-scatter.2.cloned.1.call-update
  11.5 0.0 all-gather.3.cloned.1.call-start
  11.6 0.7 rsqrt_reduce_fusion
  12.3 11.1 %reduce-scatter.2.cloned.1.call-done = f32[768,256]{1,0:T(8,128)} async-done(((f32[768,512]{1,0:T(8,128)}), f32[768,256]{1,0:T(8,128)}) %reduce-scatter.2.cloned.1.call-update) | async-done | bytes 786448 | tf_op jit(solution)/shard_map/reduce_scatter | solution.py:30
  23.4 2.2 %broadcast_multiply_fusion = f32[768,256]{1,0:T(8,128)} fusion(f32[768,256]{1,0:T(8,128)} %reduce-scatter.2.cloned.1.call-done, f32[768]{0:T(1024)S(1)} %rsqrt_reduce_fusion), kind=kLoop, calls=%fused_computation.18 | loop fusion | flops 196608 | bytes 1575936 | tf_op jit(solution)/shard_map/mul | solution.py:32
  25.6 0.0 all-gather.3.cloned.1.call-update
  25.6 0.0 all-gather.5.cloned.1.call-start
  25.7 0.7 compare_select_fusion
  26.4 0.1 reshape.133
  26.5 0.8 fusion.13
  27.2 63.3 %all-gather.3.cloned.1.call-done = f32[3072,256]{1,0:T(8,128)} async-done(((f32[768,256]{1,0:T(8,128)}), f32[3072,256]{1,0:T(8,128)}) %all-gather.3.cloned.1.call-update) | async-done | bytes 3145744 | tf_op jit(solution)/shard_map/all_gather | solution.py:32
  90.5 8.6 %gather_fusion = f32[36,256,256]{2,1,0:T(8,128)} fusion(f32[12,256,256]{2,1,0:T(8,128)} %bitcast.32, s32[1024]{0:T(1024)S(1)} %pad_clamp_fusion), kind=kCustom, calls=%fused_computation.clone | custom fusion | bytes 18874512 | tf_op jit(solution)/shard_map/jit(_take)/gather | solution.py:10
  99.1 11.0 %fusion.2 = f32[3,256,256,1]{2,1,3,0:T(8,128)S(1)} fusion(f32[3,12,256,256]{3,2,1,0:T(8,128)} %bitcast.31, f32[1,3,12,256,256]{4,3,2,1,0:T(8,128)} %param.10, f32[3,12]{1,0:T(4,128)S(1)} %get-tuple-element.6, pred[3,12]{1,0:T(4,128)(4,1)S(1)} %get-tuple-element.7), kind=kOutput, calls=%fused_computation.5 | convolution fusion | flops 3628597248 | bytes 19660980 | tf_op jit(solution)/shard_map/tkab,tkbw->taw/dot_general | solution.py:11
  110.1 1.1 fusion.10
  111.1 0.0 all-gather.5.cloned.1.call-update
  111.1 62.3 %all-gather.5.cloned.1.call-done = f32[3072,256]{1,0:T(8,128)} async-done(((f32[768,256]{1,0:T(8,128)}), f32[3072,256]{1,0:T(8,128)}) %all-gather.5.cloned.1.call-update) | async-done | bytes 3145744 | tf_op jit(solution)/shard_map/all_gather | solution.py:32
  173.5 8.6 %gather_fusion.1 = f32[36,256,256]{2,1,0:T(8,128)} fusion(f32[12,256,256]{2,1,0:T(8,128)} %bitcast.33, s32[1024]{0:T(1024)S(1)} %pad_clamp_fusion), kind=kCustom, calls=%fused_computation.1.clone | custom fusion | bytes 18874512 | tf_op jit(solution)/shard_map/jit(_take)/gather | solution.py:10
  182.0 11.0 %fusion = f32[3,256,256,1]{2,1,3,0:T(8,128)S(1)} fusion(f32[3,12,256,256]{3,2,1,0:T(8,128)} %bitcast.30, f32[1,3,12,256,256]{4,3,2,1,0:T(8,128)} %param.10, f32[3,12]{1,0:T(4,128)S(1)} %get-tuple-element.6, pred[3,12]{1,0:T(4,128)(4,1)S(1)} %get-tuple-element.7), kind=kOutput, calls=%fused_computation.3 | convolution fusion | flops 3628597248 | bytes 19660980 | tf_op jit(solution)/shard_map/tkab,tkbw->taw/dot_general | solution.py:11
  193.0 0.2 multiply_add_fusion
  193.2 0.8 copy.9
  194.0 14.7 %all_to_all.12 = f32[1,768,256]{2,0,1:T(1,128)S(1)} all-to-all(f32[1,768,256]{2,0,1:T(1,128)S(1)} %copy.9), channel_id=1, replica_groups=mesh['rel'=4,'node'=4,'feat'=2] {'rel'}, dimensions={1} | all-to-all | bytes 1572864 | tf_op jit(solution)/shard_map/all_to_all | solution.py:35
  208.8 0.9 copy.13
  (5 shorter events, 0.0 us)
Async XLA Ops:
  6.5 1.3 copy-start
  6.5 16.9 %reduce-scatter.2.cloned.1.call-start = ((), (), s32[]{:S(2)}) async-start(), calls=%async_computation.2 | async-start | bytes 2359296 | tf_op jit(solution)/shard_map/reduce_scatter | solution.py:30
  11.5 79.0 %all-gather.3.cloned.1.call-start = ((), (), s32[]{:S(2)}) async-start(), calls=%async_computation.3 | async-start | bytes 3932160 | tf_op jit(solution)/shard_map/all_gather | solution.py:32
  25.6 147.8 %all-gather.5.cloned.1.call-start = ((), (), s32[]{:S(2)}) async-start(), calls=%async_computation.4 | async-start | bytes 3932160 | tf_op jit(solution)/shard_map/all_gather | solution.py:32
  182.0 11.0 %copy-start.1 = (f32[1,256]{1,0:T(1,128)S(1)}, f32[1,256]{1,0:T(1,128)}, u32[]{:S(2)}) copy-start(f32[1,256]{1,0:T(1,128)} %param.15) | copy-start | bytes 3076
Sparse Core Ops, SparseCore 0:
  11.6 11.7 reduce-scatter.1
  25.8 64.7 all-gather.2
  111.3 62.1 all-gather.4
where the time goes:
time: 217 us; the launch traced here: 216 us
  waiting for transfers between devices  137 us (63%)
  matrix products  25.6 us (12%)
  local copies, waits for them, and re-layouts  20.3 us (9%)
  blocking collectives  14.7 us (7%)
  between operations  13.2 us (6%)
  other arithmetic  5.56 us (3%)
    all_gather x2, waiting for transfers between devices, on_device(): gathered = lax.all_gather(row_scale * current, 'node', axis=0, tiled=True)  126 us
    dot_general x2, matrix products, spread(): jnp.einsum('tkab,tkbw->taw', masked, sources, precision=lax.Precision.HIG...  21.9 us
    gather x2, local copies, waits for them, and re-layouts, spread(): sources = jnp.take(tile_rows, col_tiles, axis=0)  17.2 us
    all_to_all x1, blocking collectives, on_device(): lax.all_to_all(result[None], 'rel', split_axis=1, concat_axis=0, tiled=True)  14.7 us
    reduce_scatter x1, waiting for transfers between devices, on_device(): lax.psum_scatter(partial_sum, 'feat', scatter_dimension=1, tiled=True)  11.1 us
  transfers between devices with their start and end apart: 3, of which 3 were waited for; matrix products, arithmetic and copies ran while one was open for 1% of the time, Pallas kernels for 0%

commit v1 on v0

--- a/solution.py
+++ b/solution.py
@@ -32,7 +32,12 @@
         gathered = lax.all_gather(row_scale * current, "node", axis=0, tiled=True)
         current = row_scale * spread(gathered, masked, col_tiles)
     result = current + proj_bias[0][None, :]
-    return lax.all_to_all(result[None], "rel", split_axis=1, concat_axis=0, tiled=True)
+    return jnp.concatenate(
+        lax.all_to_all(
+            jnp.stack(jnp.split(result[None], lax.axis_size("rel"), axis=1)), "rel", 0, 0
+        ),
+        axis=0,
+    )
 
 
 def solution(mesh):

time: 217 us -> 216 us (level)
  no operation moved by 1% of the time
where the time goes in v1:
time: 216 us; the launch traced here: 215 us
  waiting for transfers between devices  137 us (63%)
  matrix products  25.6 us (12%)
  local copies, waits for them, and re-layouts  19.4 us (9%)
  blocking collectives  14.7 us (7%)
  between operations  13.2 us (6%)
  other arithmetic  5.62 us (3%)
    all_gather x2, waiting for transfers between devices, on_device(): gathered = lax.all_gather(row_scale * current, 'node', axis=0, tiled=True)  126 us
    dot_general x2, matrix products, spread(): jnp.einsum('tkab,tkbw->taw', masked, sources, precision=lax.Precision.HIG...  21.9 us
    gather x2, local copies, waits for them, and re-layouts, spread(): sources = jnp.take(tile_rows, col_tiles, axis=0)  17.2 us
    all_to_all x1, blocking collectives, on_device(): lax.all_to_all(jnp.stack(jnp.split(result[None], lax.axis_size('rel'), ax...  14.7 us
    reduce_scatter x1, waiting for transfers between devices, on_device(): lax.psum_scatter(partial_sum, 'feat', scatter_dimension=1, tiled=True)  11.1 us
  transfers between devices with their start and end apart: 3, of which 3 were waited for; matrix products, arithmetic and copies ran while one was open for 1% of the time, Pallas kernels for 0%

profile of v1, /device:TPU:0, one launch (start us, length us, event | category | flops | bytes accessed | tf_op | source)
XLA Modules:
  0.0 215.5 jit_solution(13550042795787411703)
XLA Ops:
  6.5 1.3 copy-done
  7.8 3.7 %fusion.11 = f32[768,512]{1,0:T(8,128)} fusion(f32[768,384]{1,0:T(8,128)S(1)} %copy-done, f32[1,384,512]{2,1,0:T(8,128)} %param.14), kind=kOutput, calls=%fused_computation.16 | convolution fusion | flops 905969664 | bytes 3538944 | tf_op jit(solution)/shard_map/dot_general | solution.py:27
  11.5 0.0 reduce-scatter.2.cloned.1.call-update
  11.5 0.0 all-gather.3.cloned.1.call-start
  11.6 0.7 rsqrt_reduce_fusion
  12.3 11.1 %reduce-scatter.2.cloned.1.call-done = f32[768,256]{1,0:T(8,128)} async-done(((f32[768,512]{1,0:T(8,128)}), f32[768,256]{1,0:T(8,128)}) %reduce-scatter.2.cloned.1.call-update) | async-done | bytes 786448 | tf_op jit(solution)/shard_map/reduce_scatter | solution.py:30
  23.4 2.2 %broadcast_multiply_fusion = f32[768,256]{1,0:T(8,128)} fusion(f32[768,256]{1,0:T(8,128)} %reduce-scatter.2.cloned.1.call-done, f32[768]{0:T(1024)S(1)} %rsqrt_reduce_fusion), kind=kLoop, calls=%fused_computation.19 | loop fusion | flops 196608 | bytes 1575936 | tf_op jit(solution)/shard_map/mul | solution.py:32
  25.6 0.0 all-gather.5.cloned.1.call-start
  25.7 0.7 compare_select_fusion
  26.4 0.1 reshape.134
  26.5 0.8 fusion.13
  27.2 63.3 %all-gather.3.cloned.1.call-done = f32[3072,256]{1,0:T(8,128)} async-done(((f32[768,256]{1,0:T(8,128)}), f32[3072,256]{1,0:T(8,128)}) %all-gather.3.cloned.1.call-update) | async-done | bytes 3145744 | tf_op jit(solution)/shard_map/all_gather | solution.py:32
  90.5 8.6 %gather_fusion = f32[36,256,256]{2,1,0:T(8,128)} fusion(f32[12,256,256]{2,1,0:T(8,128)} %bitcast.40, s32[1024]{0:T(1024)S(1)} %pad_clamp_fusion), kind=kCustom, calls=%fused_computation.clone | custom fusion | bytes 18874512 | tf_op jit(solution)/shard_map/jit(_take)/gather | solution.py:10
  99.1 11.0 %fusion.2 = f32[3,256,256,1]{2,1,3,0:T(8,128)S(1)} fusion(f32[3,12,256,256]{3,2,1,0:T(8,128)} %bitcast.39, f32[1,3,12,256,256]{4,3,2,1,0:T(8,128)} %param.10, f32[3,12]{1,0:T(4,128)S(1)} %get-tuple-element.10, pred[3,12]{1,0:T(4,128)(4,1)S(1)} %get-tuple-element.11), kind=kOutput, calls=%fused_computation.5 | convolution fusion | flops 3628597248 | bytes 19660980 | tf_op jit(solution)/shard_map/tkab,tkbw->taw/dot_general | solution.py:11
  110.1 1.1 fusion.10
  111.1 0.0 all-gather.5.cloned.1.call-update
  111.1 62.3 %all-gather.5.cloned.1.call-done = f32[3072,256]{1,0:T(8,128)} async-done(((f32[768,256]{1,0:T(8,128)}), f32[3072,256]{1,0:T(8,128)}) %all-gather.5.cloned.1.call-update) | async-done | bytes 3145744 | tf_op jit(solution)/shard_map/all_gather | solution.py:32
  173.5 8.6 %gather_fusion.1 = f32[36,256,256]{2,1,0:T(8,128)} fusion(f32[12,256,256]{2,1,0:T(8,128)} %bitcast.41, s32[1024]{0:T(1024)S(1)} %pad_clamp_fusion), kind=kCustom, calls=%fused_computation.1.clone | custom fusion | bytes 18874512 | tf_op jit(solution)/shard_map/jit(_take)/gather | solution.py:10
  182.0 11.0 %fusion = f32[3,256,256,1]{2,1,3,0:T(8,128)S(1)} fusion(f32[3,12,256,256]{3,2,1,0:T(8,128)} %bitcast.38, f32[1,3,12,256,256]{4,3,2,1,0:T(8,128)} %param.10, f32[3,12]{1,0:T(4,128)S(1)} %get-tuple-element.10, pred[3,12]{1,0:T(4,128)(4,1)S(1)} %get-tuple-element.11), kind=kOutput, calls=%fused_computation.3 | convolution fusion | flops 3628597248 | bytes 19660980 | tf_op jit(solution)/shard_map/tkab,tkbw->taw/dot_general | solution.py:11
  193.0 0.2 multiply_add_fusion
  193.2 0.1 slice_bitcast_fusion.3
  193.3 0.1 pad_maximum_fusion
  193.3 14.7 %all_to_all.5 = f32[4,1,192,256]{3,2,1,0:T(8,128)S(1)} all-to-all(f32[4,1,192,256]{3,2,1,0:T(8,128)S(1)} %pad_maximum_fusion), channel_id=1, replica_groups=mesh['rel'=4,'node'=4,'feat'=2] {'rel'}, dimensions={0} | all-to-all | bytes 1572864 | tf_op jit(solution)/shard_map/all_to_all | solution.py:36
  208.1 0.9 copy.18
  (6 shorter events, 0.0 us)
Async XLA Ops:
  6.5 1.3 copy-start
  6.5 16.9 %reduce-scatter.2.cloned.1.call-start = ((), (), s32[]{:S(2)}) async-start(), calls=%async_computation.2 | async-start | bytes 2359296 | tf_op jit(solution)/shard_map/reduce_scatter | solution.py:30
  11.5 79.0 %all-gather.3.cloned.1.call-start = ((), (), s32[]{:S(2)}) async-start(), calls=%async_computation.3 | async-start | bytes 3932160 | tf_op jit(solution)/shard_map/all_gather | solution.py:32
  25.6 147.8 %all-gather.5.cloned.1.call-start = ((), (), s32[]{:S(2)}) async-start(), calls=%async_computation.4 | async-start | bytes 3932160 | tf_op jit(solution)/shard_map/all_gather | solution.py:32
  182.0 11.0 %copy-start.1 = (f32[1,256]{1,0:T(1,128)S(1)}, f32[1,256]{1,0:T(1,128)}, u32[]{:S(2)}) copy-start(f32[1,256]{1,0:T(1,128)} %param.15) | copy-start | bytes 3076
Sparse Core Ops, SparseCore 0:
  11.6 11.7 reduce-scatter.1
  25.7 64.7 all-gather.2
  111.3 62.1 all-gather.4
